TPU v7x, 512 devices: a whole 4x4x16 slice. The times are simulated.
512 devices in a mesh: row: 16 (over z), col: 32 (over y, x, core).
Axes of the slice: x: 4, y: 4, z: 16, core: 2. Of those that a mesh axis runs over, the one named last changes fastest.
Arguments:
- eigvecs: bfloat16 [8192, 16384], P('row', 'col'), may hold values from -0.01171875 to 0.01171875
- pole_order: int32 [16384], P('col'), may hold values from 0 to 16383, as said below
- pole_weight: float32 [16384], P('col'), may hold values from 0.17 to 6
- root_gap: int32 [2048], replicated, may hold values from 1024 to 15358, as said below
- root_shift: float32 [2048], replicated, may hold values from -0.25 to 0.25
- column_weight: float32 [2048], replicated, may hold values from 4 to 40
- panel_vectors: bfloat16 [2, 8192, 256], P(None, 'row'), may hold values from -0.0625 to 0.0625
- panel_factors: float32 [2, 256, 256], replicated, as said below
Outputs:
- eigenvectors: bfloat16 [8192, 2048], P('row', 'col')
Inputs may be any that keep to these rules, and one draw needn't show every extreme that they name: `pole_order`: each value appears once. Distinct values; root j lies strictly between the poles at 2 * root_gap[j] and 2 * root_gap[j] + 2. `panel_factors`: upper triangular, with a diagonal between 2 and 4.
All inputs are finite; a program needn't handle non-finite values.
Results may differ from a plain program's by a relative error of at most 0.02.
Values may be sent and summed in bfloat16 or wider, within the bound.
A program may use at most 64 MiB of HBM per device.

v0:
```python
import jax
import jax.numpy as jnp
from jax import lax
from jax.sharding import PartitionSpec as P


def split_up(shard, dim, devices):
    before, after = (shard.shape[:dim], shard.shape[dim + 1 :])
    return jnp.moveaxis(shard.reshape(*before, devices, -1, *after), dim, 0)


def sent_and_summed(shard, axis, dim):
    devices = lax.axis_size(axis)
    blocks = lax.all_to_all(split_up(shard, dim, devices), axis, 0, 0, tiled=True)
    return jnp.sum(blocks.astype(jnp.float32), axis=0)


def gathered_total(shard, axis):
    blocks = lax.all_gather(shard, axis).astype(jnp.float32)
    return blocks.sum(axis=0)


def cauchy_values(pole_values, weight_slice, root_gap, root_shift, column_weight):
    root_values = 2.0 * root_gap.astype(jnp.float32) + 1.0 + root_shift
    numer = weight_slice[:, None] * column_weight[None, :]
    return (numer / (pole_values[:, None] - root_values[None, :])).astype(jnp.bfloat16)


def shards(
    eigvecs,
    pole_order,
    pole_weight,
    root_gap,
    root_shift,
    column_weight,
    panel_vectors,
    panel_factors,
):
    matrix = cauchy_values(
        2.0 * pole_order.astype(jnp.float32), pole_weight, root_gap, root_shift, column_weight
    )
    partial_value = jnp.dot(eigvecs, matrix, preferred_element_type=jnp.float32)
    owned = sent_and_summed(partial_value.astype(jnp.bfloat16), "col", 1).astype(jnp.bfloat16)
    cyclic = lax.all_to_all(owned, "row", split_axis=0, concat_axis=0, tiled=True)
    current = cyclic.astype(jnp.float32)
    for panel_index in range(panel_vectors.shape[0]):
        vectors = panel_vectors[panel_index].astype(jnp.float32)
        project_local = jnp.einsum("rp,rc->pc", vectors, current)
        project = gathered_total(project_local.astype(jnp.bfloat16), "row").astype(jnp.float32)
        factored = jnp.dot(panel_factors[panel_index], project)
        current = current - jnp.dot(vectors, factored)
    return current.astype(jnp.bfloat16)


def solution(mesh):
    return jax.shard_map(
        shards,
        mesh=mesh,
        in_specs=(P("row", "col"), P("col"), P("col"), P(), P(), P(), P(None, "row", None), P()),
        out_specs=P("row", "col"),
        check_vma=False,
    )
```

profile of v0, /device:TPU:32, one launch (start us, length us, event | category | flops | bytes accessed | tf_op | source)
XLA Modules:
  0.0 131.2 jit_solution(9917853317564819776)
XLA Ops:
  0.0 0.0 copy-start
  0.0 0.7 convert_multiply_fusion
  0.7 0.7 add_add_fusion
  1.5 0.0 copy-done
  1.5 2.2 %convolution_convert_fusion = bf16[2048,512]{1,0:T(8,128)(2,1)S(1)} fusion(bf16[512,512]{1,0:T(8,128)(2,1)S(1)} %copy-done, f32[2048]{0:T(1024)S(1)} %add_add_fusion, f32[512]{0:T(512)S(1)} %convert_multiply_fusion, f32[2048]{0:T(1024)} %param.13, f32[512]{0:T(512)} %param.10), kind=kOutput, calls=%fused_computation.1 | convolution fusion | flops 1078984704 | bytes 2641920 | tf_op jit(solution)/shard_map/dot_general | solution.py:42
  3.7 35.6 %all_to_all.17 = bf16[32,512,64]{1,2,0:T(8,128)(2,1)S(1)} all-to-all(bf16[32,512,64]{1,2,0:T(8,128)(2,1)S(1)} %bitcast.56), channel_id=1, replica_groups=mesh['row'=16,'col'=32] {'col'}, dimensions={0} | all-to-all | bytes 4194304 | tf_op jit(solution)/shard_map/all_to_all | solution.py:14
  39.3 0.0 copy-start.1
  39.3 0.3 reduce_sum.30
  39.6 0.1 copy.10
  39.7 0.1 reshape.14
  39.8 27.1 %all_to_all.18 = bf16[16,2,1024]{2,1,0:T(2,128)(2,1)S(1)} all-to-all(bf16[16,2,1024]{2,1,0:T(2,128)(2,1)S(1)} %reshape.14), channel_id=1, replica_groups=mesh['row'=16,'col'=32] {'row'}, dimensions={0} | all-to-all | bytes 131072 | tf_op jit(solution)/shard_map/all_to_all | solution.py:44
  66.9 0.1 reshape.15
  67.1 0.1 copy.11
  67.2 0.0 copy-done.1
  67.2 0.2 fusion.11
  67.4 30.5 %all-gather = bf16[4096,64]{0,1:T(8,128)(2,1)S(1)} all-gather(bf16[256,64]{0,1:T(8,128)(2,1)S(1)} %fusion.11), channel_id=2, replica_groups=mesh['row'=16,'col'=32] {'row'}, dimensions={0}, use_global_device_ids=true | all-gather | bytes 557056 | tf_op jit(solution)/shard_map/all_gather | solution.py:19
  97.9 0.0 copy-start.2
  97.9 0.1 convert_element_type.56
  98.0 0.3 copy.12
  98.3 0.2 bitcast_reduce_fusion.1
  98.5 0.5 copy-done.2
  98.9 0.4 fusion.4
  99.3 0.2 fusion.12
  99.5 30.2 %all-gather.1 = bf16[4096,64]{0,1:T(8,128)(2,1)S(1)} all-gather(bf16[256,64]{0,1:T(8,128)(2,1)S(1)} %fusion.12), channel_id=3, replica_groups=mesh['row'=16,'col'=32] {'row'}, dimensions={0}, use_global_device_ids=true | all-gather | bytes 557056 | tf_op jit(solution)/shard_map/all_gather | solution.py:19
  129.7 0.1 convert_element_type.57
  129.7 0.3 copy.13
  130.1 0.2 bitcast_reduce_fusion
  130.2 1.0 fusion.6
Async XLA Ops:
  0.0 1.5 %copy-start = (bf16[512,512]{1,0:T(8,128)(2,1)S(1)}, bf16[512,512]{1,0:T(8,128)(2,1)}, u32[]{:S(2)}) copy-start(bf16[512,512]{1,0:T(8,128)(2,1)} %param.8) | copy-start | bytes 1572868
  39.3 27.9 %copy-start.1 = (bf16[2,512,256]{2,1,0:T(8,128)(2,1)S(1)}, bf16[2,512,256]{2,1,0:T(8,128)(2,1)}, u32[]{:S(2)}) copy-start(bf16[2,512,256]{2,1,0:T(8,128)(2,1)} %param.14) | copy-start | bytes 1572868
  97.9 1.0 copy-start.2
where the time goes:
time: 132 us; the launch traced here: 131 us
  blocking collectives  123 us (93%)
  matrix products  3.99 us (3%)
  other arithmetic  2.22 us (2%)
  local copies, waits for them, and re-layouts  1.62 us (1%)
    all_gather x2, blocking collectives, gathered_total(): blocks = lax.all_gather(shard, axis).astype(jnp.float32)  60.7 us
    all_to_all x1, blocking collectives, sent_and_summed(): lax.all_to_all(split_up(shard, dim, devices), axis, 0, 0, tiled=True)  35.6 us
    all_to_all x1, blocking collectives, shards(): lax.all_to_all(owned, 'row', split_axis=0, concat_axis=0, tiled=True)  27.1 us

commit v1 on v0

v1 whole, which is shorter than its diff:
```python
import functools

import jax
import jax.numpy as jnp
from jax import lax
from jax.experimental import pallas as pl
from jax.experimental.pallas import tpu as pltpu
from jax.sharding import PartitionSpec as P

MESH = pl.DeviceIdType.MESH
F32, BF16 = jnp.float32, jnp.bfloat16
NZ, NX, NY = 16, 4, 4
NQ = NX * NY
DIST = [8] + [s * d for d in range(7, 0, -1) for s in (1, -1)] + [0]
OFFS = sorted(
    ((dy, dx) for dy in range(NY) for dx in range(NX) if (dy, dx) != (0, 0)),
    key=lambda o: -(min(o[0], NY - o[0]) + min(o[1], NX - o[1])),
)
NT = 4
TA = (((0,), (0,)), ((), ()))


def dot(a, b):
    return jnp.dot(a, b, preferred_element_type=F32)


def kernel(
    a_hbm, order_ref, weight_ref, gap_ref, shift_ref, cw_ref, v_hbm, t_hbm, out_ref,
    a_buf, v_buf, t_buf, pole_b, weight_b, cau, psend, pown, precv, rsend, rrecv, mz, cbuf,
    gf, gs, gr, gall, pf, ps, pr, pall,
    load_sem, pair_s, pair_r, rs_s, rs_r, z_sem, x_sem, g_sem, gx_sem, p_sem,
):
    z = lax.axis_index("row")
    c = lax.axis_index("col")
    core = lax.rem(c, 2)
    q = c // 2
    x, y = lax.rem(q, NX), q // NX
    mate = (z, c + 1 - 2 * core)

    def zpeer(d):
        return lax.rem(z + d + NZ, NZ)

    def chip(off):
        return lax.rem(y + off[0], NY) * NX + lax.rem(x + off[1], NX)

    def send(src, dst, ssem, rsem, dev):
        pltpu.make_async_remote_copy(
            src_ref=src, dst_ref=dst, send_sem=ssem, recv_sem=rsem, device_id=dev, device_id_type=MESH
        ).start()

    def wait(ref, sem):
        pltpu.make_async_copy(ref, ref, sem).wait()

    for j, d in enumerate(DIST):
        for h in range(2):
            half = (1 - core) if h == 0 else core
            start = pl.multiple_of(zpeer(d) * 32 + half * 16, 16)
            pltpu.make_async_copy(
                a_hbm.at[pl.ds(start, 16), :], a_buf.at[j // 4, h, j % 4], load_sem.at[0]
            ).start()
    pltpu.make_async_copy(v_hbm, v_buf, load_sem.at[1]).start()
    pltpu.make_async_copy(t_hbm, t_buf, load_sem.at[2]).start()

    barrier = pltpu.get_barrier_semaphore()
    peers = [(zpeer(d), c) for d in DIST if d] + [(z, chip(o) * 2 + core) for o in OFFS] + [mate]
    for dev in peers:
        pl.semaphore_signal(barrier, inc=1, device_id=dev, device_id_type=MESH)

    for b in range(4):
        lanes = pl.ds(b * 128, 128)
        pole = 2.0 * order_ref[:, lanes].astype(F32)
        pole_b[b] = jnp.broadcast_to(pole, (128, 128)).T
        weight_b[b] = jnp.broadcast_to(weight_ref[:, lanes], (128, 128)).T

    wait(a_buf, load_sem.at[0])

    @pl.loop(0, 8)
    def _(n):
        for e in range(2):
            lanes = pl.ds(pl.multiple_of(n * 256 + e * 128, 128), 128)
            root = 2.0 * gap_ref[:, lanes].astype(F32) + 1.0 + shift_ref[:, lanes]
            for b in range(4):
                cau[b * 128 : b * 128 + 128, e * 128 : e * 128 + 128] = (
                    weight_b[b] / (pole_b[b] - root)
                ).astype(BF16)
        part = dot(a_buf[...].reshape(512, 512), cau[...])
        for t in range(NT):
            for e in range(2):
                lanes = slice(e * 128, e * 128 + 128)
                psend[t, 2 * n + e] = part[t * 128 : t * 128 + 64, lanes].astype(BF16)
                pown[t, 2 * n + e] = part[t * 128 + 64 : t * 128 + 128, lanes]

    wait(v_buf, load_sem.at[1])
    mine = pl.ds(pl.multiple_of(core * 128, 128), 128)
    gram = lax.dot_general(v_buf[1], v_buf[0, :, mine], TA, preferred_element_type=F32)
    gf[...] = gram.reshape(NZ, 16, 128)
    gs[...] = gram.reshape(NZ, 16, 128).astype(BF16)

    pl.semaphore_wait(barrier, len(peers))

    for t in range(NT):
        send(psend.at[t], precv.at[t], pair_s.at[t], pair_r.at[t], mate)
    for j, d in enumerate(DIST[:-1]):
        send(gs.at[zpeer(d)], gr.at[j], g_sem.at[0], g_sem.at[1], (zpeer(d), c))

    for t in range(NT):
        wait(precv.at[t], pair_r.at[t])

        @pl.loop(0, NQ)
        def _(n, t=t):
            rsend[t, n] = (pown[t, n] + precv[t, n].astype(F32)).astype(BF16)

        for j, o in enumerate(OFFS):
            dest = chip(o)
            send(rsend.at[t, dest], rrecv.at[t, j], rs_s.at[t], rs_r.at[t], (z, dest * 2 + core))

    wait(gr, g_sem.at[1])
    total = gf[z]
    for j in range(NZ - 1):
        total += gr[j].astype(F32)
    gall[core, z] = total.astype(BF16)
    for d in DIST[:-1]:
        send(gall.at[core, z], gall.at[core, z], g_sem.at[2], g_sem.at[3], (zpeer(d), c))

    scale = cw_ref[:, pl.ds(pl.multiple_of(q * 128, 128), 128)]
    for t in range(NT):
        wait(rrecv.at[t], rs_r.at[t])
        total = pown[t, q] + precv[t, q].astype(F32)
        for j in range(NQ - 1):
            total += rrecv[t, j].astype(F32)
        merged = (total * scale).astype(BF16)
        for i in range(4):
            d = DIST[4 * t + i]
            if d:
                mz[t, i] = merged[i * 16 : i * 16 + 16]
            else:
                cbuf[core, z] = merged[i * 16 : i * 16 + 16]
        for i in range(4):
            d = DIST[4 * t + i]
            if d:
                send(mz.at[t, i], cbuf.at[core, z], z_sem.at[0], z_sem.at[1], (zpeer(d), c))

    wait(gall.at[0, pl.ds(0, NZ - 1)], g_sem.at[3])
    send(gall.at[core], gall.at[core], gx_sem.at[0], gx_sem.at[1], mate)

    wait(cbuf.at[0, pl.ds(0, NZ - 1)], z_sem.at[1])
    send(cbuf.at[core], cbuf.at[core], x_sem.at[0], x_sem.at[1], mate)
    wait(cbuf.at[0], x_sem.at[1])

    cur = jnp.concatenate([cbuf[k, r] for r in range(NZ) for k in range(2)], axis=0).astype(F32)
    lane = lax.broadcasted_iota(jnp.int32, (512, 128), 1)
    own = jnp.where(lane // 64 == core, cur, pltpu.roll(cur, 64, 1))
    own16 = own.astype(BF16)
    first = lax.dot_general(v_buf[0], own16, TA, preferred_element_type=F32)
    second = lax.dot_general(v_buf[1], own16, TA, preferred_element_type=F32)
    low = lax.broadcasted_iota(jnp.int32, (256, 128), 1) < 64
    proj = jnp.where(low, first, second).reshape(NZ, 16, 128)
    pf[...] = proj
    ps[...] = proj.astype(BF16)
    for j, d in enumerate(DIST[:-1]):
        send(ps.at[zpeer(d)], pr.at[j], p_sem.at[0], p_sem.at[1], (zpeer(d), c))
    wait(pr, p_sem.at[1])
    total = pf[z]
    for j in range(NZ - 1):
        total += pr[j].astype(F32)
    pall[z] = total.astype(BF16)
    for d in DIST[:-1]:
        send(pall.at[z], pall.at[z], p_sem.at[2], p_sem.at[3], (zpeer(d), c))
    wait(t_buf, load_sem.at[2])
    wait(gall.at[0], gx_sem.at[1])
    wait(pall.at[pl.ds(0, NZ - 1)], p_sem.at[3])

    proj16 = pall[...].reshape(256, 128)
    f1 = dot(t_buf[0].astype(BF16), proj16).astype(BF16)
    corr = dot(gall[0].reshape(256, 128), f1[:128]) + dot(gall[1].reshape(256, 128), f1[128:])
    rest = pltpu.roll(proj16.astype(F32), 64, 1) - corr
    f2 = dot(t_buf[1].astype(BF16), rest.astype(BF16)).astype(BF16)
    res = own - dot(v_buf[0], f1) - dot(v_buf[1], f2)
    for b in range(4):
        out_ref[:, b * 128 : b * 128 + 128] = res[b * 128 : b * 128 + 128].T[:64].astype(BF16)

    for t in range(NT):
        wait(psend.at[t], pair_s.at[t])
        wait(rrecv.at[t], rs_s.at[t])
    wait(gr, g_sem.at[0])
    wait(gr, g_sem.at[2])
    wait(gall.at[0], gx_sem.at[0])
    wait(gr, z_sem.at[0])
    wait(cbuf.at[0], x_sem.at[0])
    wait(pr, p_sem.at[0])
    wait(pr, p_sem.at[2])


def shards(a, order, weight, gap, shift, cw, v, t):
    vmem = pl.BlockSpec(memory_space=pltpu.VMEM)
    hbm = pl.BlockSpec(memory_space=pl.ANY)
    dma = pltpu.SemaphoreType.DMA
    out = pl.pallas_call(
        kernel,
        out_shape=jax.ShapeDtypeStruct((64, 512), BF16),
        in_specs=[hbm, vmem, vmem, vmem, vmem, vmem, hbm, hbm],
        out_specs=vmem,
        scratch_shapes=[
            pltpu.VMEM((NT, 2, 4, 16, 512), BF16),
            pltpu.VMEM((2, 512, 256), BF16),
            pltpu.VMEM((2, 256, 256), F32),
            pltpu.VMEM((4, 128, 128), F32),
            pltpu.VMEM((4, 128, 128), F32),
            pltpu.VMEM((512, 256), BF16),
            pltpu.VMEM((NT, NQ, 64, 128), BF16),
            pltpu.VMEM((NT, NQ, 64, 128), F32),
            pltpu.VMEM((NT, NQ, 64, 128), BF16),
            pltpu.VMEM((NT, NQ, 64, 128), BF16),
            pltpu.VMEM((NT, NQ - 1, 64, 128), BF16),
            pltpu.VMEM((NT, 4, 16, 128), BF16),
            pltpu.VMEM((2, NZ, 16, 128), BF16),
            pltpu.VMEM((NZ, 16, 128), F32),
            pltpu.VMEM((NZ, 16, 128), BF16),
            pltpu.VMEM((NZ - 1, 16, 128), BF16),
            pltpu.VMEM((2, NZ, 16, 128), BF16),
            pltpu.VMEM((NZ, 16, 128), F32),
            pltpu.VMEM((NZ, 16, 128), BF16),
            pltpu.VMEM((NZ - 1, 16, 128), BF16),
            pltpu.VMEM((NZ, 16, 128), BF16),
            dma((3,)), dma((NT,)), dma((NT,)), dma((NT,)), dma((NT,)),
            dma((2,)), dma((2,)), dma((4,)), dma((2,)), dma((4,)),
        ],
        compiler_params=pltpu.CompilerParams(collective_id=0, has_side_effects=True),
    )(
        a, order.reshape(1, -1), weight.reshape(1, -1), gap.reshape(1, -1), shift.reshape(1, -1),
        cw.reshape(1, -1), v, t,
    )
    return out.T


def solution(mesh):
    return jax.shard_map(
        shards,
        mesh=mesh,
        in_specs=(P("row", "col"), P("col"), P("col"), P(), P(), P(), P(None, "row", None), P()),
        out_specs=P("row", "col"),
        check_vma=False,
    )
```

time: 132 us -> 54.5 us (0.41)
  the two profiles are of different devices: /device:TPU:32 before, /device:TPU:1 now
where the time goes in v1:
time: 54.5 us; the launch traced here: 54.3 us
  Pallas kernels  52.8 us (97%)
  local copies, waits for them, and re-layouts  1.47 us (3%)
    pallas_call x1, Pallas kernels, shards(): pl.pallas_call(kernel, out_shape=jax.ShapeDtypeStruct((64, 512), BF16), i...  52.8 us
    unnamed x1, local copies, waits for them, and re-layouts  1.47 us

profile of v1, /device:TPU:1, one launch (start us, length us, event | category | flops | bytes accessed | tf_op | source)
XLA Modules:
  0.0 54.3 jit_solution(339462593740114803)
XLA Ops:
  0.0 52.8 %shard_map.82 = bf16[64,512]{1,0:T(8,128)(2,1)} custom-call(bf16[512,512]{1,0:T(8,128)(2,1)} %a_hbm.1, s32[1,512]{1,0:T(1,128)} %bitcast.10, f32[1,512]{1,0:T(1,128)} %bitcast.11, s32[1,2048]{1,0:T(1,128)} %bitcast.7, f32[1,2048]{1,0:T(1,128)} %bitcast.8, f32[1,2048]{1,0:T(1,128)} %bitcast.9, bf16[2,512,256]{2,1,0:T(8,128)(2,1)} %v_hbm.1, f32[2,256,256]{2,1,0:T(8,128)} %t_hbm.1), custom_call_target="tpu_custom_call" | custom-call | tf_op jit(solution)/shard_map/pallas_call | solution.py:198
  52.8 1.5 %copy.10 = bf16[512,64]{0,1:T(8,128)(2,1)} copy(bf16[512,64]{0,1:T(8,128)(2,1)} %bitcast.6) | data formatting | bytes 131072

commit v2 on v0

v2 whole, which is shorter than its diff:
```python
import jax
import jax.numpy as jnp
from jax import lax
from jax.experimental import pallas as pl
from jax.experimental.pallas import tpu as pltpu
from jax.sharding import PartitionSpec as P

MESH = pl.DeviceIdType.MESH
F32, BF16 = jnp.float32, jnp.bfloat16
NZ, NX, NY = 16, 4, 4
NQ = NX * NY
DIST = [8] + [s * d for d in range(7, 0, -1) for s in (1, -1)] + [0]
NEAR = [4, 3, -3, 2, -2, 1, -1]
NT = 4
TA = (((0,), (0,)), ((), ()))


def dot(a, b):
    return jnp.dot(a, b, preferred_element_type=F32)


def kernel(
    a_hbm, order_hbm, weight_hbm, gap_hbm, shift_hbm, cw_hbm, v_hbm, t_hbm, out_ref,
    order_ref, weight_ref, gap_ref, shift_ref, cw_ref, a_buf, v_buf, t_buf, vt,
    pole_b, weight_b, cau, part, precv, s1, r1, s2, r2, mz, cbuf,
    gf, gsum, gin, gall, w1, w2, own_t, pf, ps, pr, pall,
    load_sem, pair_s, pair_r, s1_s, s1_r, s2_s, s2_r, z_sem, g_sem, gx_sem, p_sem, tok,
):
    z = lax.axis_index("row")
    c = lax.axis_index("col")
    core = c & 1
    q = c >> 1
    x, y = q & (NX - 1), q >> 2
    mate = (z, c + 1 - 2 * core)

    def zpeer(d):
        return (z + d + NZ) & (NZ - 1)

    def xchip(d):
        return (y * NX + ((x + d) & (NX - 1))) * 2 + core

    def ychip(d):
        return (((y + d) & (NY - 1)) * NX + x) * 2 + core

    def send(src, dst, ssem, rsem, dev):
        pltpu.make_async_remote_copy(
            src_ref=src, dst_ref=dst, send_sem=ssem, recv_sem=rsem, device_id=dev, device_id_type=MESH
        ).start()

    def wait(ref, sem):
        pltpu.make_async_copy(ref, ref, sem).wait()

    small = [
        (order_hbm, order_ref), (weight_hbm, weight_ref), (gap_hbm, gap_ref),
        (shift_hbm, shift_ref), (cw_hbm, cw_ref),
    ]
    for i, (src, dst) in enumerate(small):
        pltpu.make_async_copy(src, dst, load_sem.at[3 + i]).start()
    barrier = pltpu.get_barrier_semaphore()
    peers = [mate]
    for d in (1, 2, 3):
        peers += [(z, xchip(d)), (z, ychip(d))]
    peers += [(zpeer(d), c) for d in (1, -1)]
    for dev in peers:
        pl.semaphore_signal(barrier, inc=1, device_id=dev, device_id_type=MESH)

    for j, d in enumerate(DIST):
        pltpu.make_async_copy(a_hbm.at[zpeer(d)], a_buf.at[j // 4, :, j % 4], load_sem.at[0]).start()

    for i in range(4):
        wait(small[i][1], load_sem.at[3 + i])
    pltpu.make_async_copy(v_hbm, v_buf, load_sem.at[1]).start()
    pltpu.make_async_copy(t_hbm, t_buf, load_sem.at[2]).start()
    for b in range(4):
        lanes = pl.ds(b * 128, 128)
        pole = 2.0 * order_ref[:, lanes].astype(F32)
        pole_b[b] = jnp.broadcast_to(pole, (128, 128)).T
        weight_b[b] = jnp.broadcast_to(weight_ref[:, lanes], (128, 128)).T

    root = 2.0 * gap_ref[...].astype(F32) + 1.0 + shift_ref[...]
    turned_root = pltpu.roll(root, 64, 1)
    left1 = lax.broadcasted_iota(jnp.int32, (1, 128), 1) < 64

    def cauchy(n):
        for e in range(4):
            b0 = 2 * (4 * (n % 2) + e)
            if n < 2:
                lanes = jnp.where(left1, root[b0 : b0 + 1], turned_root[b0 + 1 : b0 + 2])
            else:
                lanes = jnp.where(left1, turned_root[b0 : b0 + 1], root[b0 + 1 : b0 + 2])
            for b in range(4):
                cau[n, b * 128 : b * 128 + 128, e * 128 : e * 128 + 128] = (
                    weight_b[b] / (pole_b[b] - lanes)
                ).astype(BF16)

    for n in range(4):
        cauchy(n)
    wait(a_buf, load_sem.at[0])
    for t in range(NT):
        for n in range(4):
            prod = dot(a_buf[t].reshape(128, 512), cau[n]).astype(BF16)
            for e in range(4):
                part[n // 2, t, 4 * (n % 2) + e] = prod[:, e * 128 : e * 128 + 128]
        if t == 0:
            pl.semaphore_wait(barrier, len(peers))
        send(part.at[1 - core, t], precv.at[t], pair_s.at[t], pair_r.at[t], mate)
    token(tok, 0, (1, -1), zpeer, c)

    wait(v_buf, load_sem.at[1])
    mine = pl.ds(pl.multiple_of(core * 128, 128), 128)
    gram = lax.dot_general(v_buf[1], v_buf[0, :, mine], TA, preferred_element_type=F32)
    gf[...] = gram.reshape(NQ, 16, 128)
    gsum[0] = gf[q]

    def gram_send(i):
        for j in range(3):
            to = zpeer((1 - 2 * core) * (j + 1) * 4**i)
            send(gsum.at[i], gin.at[i, j], g_sem.at[i], g_sem.at[2 + i], (to, c))

    def gram_add(i):
        wait(gin.at[i], g_sem.at[2 + i])
        gsum[i + 1] = gsum[i] + gin[i, 0] + gin[i, 1] + gin[i, 2]

    left64 = lax.broadcasted_iota(jnp.int32, (64, 128), 1) < 64

    def first_phase(t):
        wait(precv.at[t], pair_r.at[t])

        @pl.loop(0, NY)
        def _(yy):
            for e in range(2):
                total = part[core, t, 2 * yy + e].astype(F32) + precv[t, 2 * yy + e].astype(F32)
                turned = pltpu.roll(total, 64, 1)
                even = jnp.where(left64, total[:64], turned[64:]).astype(BF16)
                odd = jnp.where(left64, turned[:64], total[64:]).astype(BF16)
                for xx, packed in ((2 * e, even), (2 * e + 1, odd)):
                    s1[t, 0, xx, yy] = packed[:32]
                    s1[t, 1, yy, xx] = packed[32:]

    def first_sends(t, ds):
        for d in ds:
            send(s1.at[t, 0, (x + d) & (NX - 1)], r1.at[t, 0, d - 1], s1_s.at[t], s1_r.at[t], (z, xchip(d)))
            send(s1.at[t, 1, (y + d) & (NY - 1)], r1.at[t, 1, d - 1], s1_s.at[t], s1_r.at[t], (z, ychip(d)))

    def second_phase(t):
        wait(r1.at[t], s1_r.at[t])
        for h, me in ((0, x), (1, y)):
            total = s1[t, h, me].astype(F32)
            for j in range(3):
                total += r1[t, h, j].astype(F32)
            s2[t, h] = total.astype(BF16)
        for d in (2, 1, 3):
            send(s2.at[t, 0, ((y + d) & (NY - 1))], r2.at[t, 0, d - 1], s2_s.at[t], s2_r.at[t], (z, ychip(d)))
            send(s2.at[t, 1, ((x + d) & (NX - 1))], r2.at[t, 1, d - 1], s2_s.at[t], s2_r.at[t], (z, xchip(d)))

    def exchange(t):
        wait(r2.at[t], s2_r.at[t])
        for h, me in ((0, y), (1, x)):
            total = s2[t, h, me].astype(F32)
            for j in range(3):
                total += r2[t, h, j].astype(F32)
            mz[t, 2 * h : 2 * h + 2] = (total * scale).astype(BF16).reshape(2, 16, 128)
        for i in range(4):
            d = DIST[4 * t + i]
            if d:
                send(mz.at[t, i], cbuf.at[z], z_sem.at[0], z_sem.at[1], (zpeer(d), c))
            else:
                cbuf[z] = mz[t, i]

    first_phase(0)
    first_sends(0, (2, 1, 3))
    first_phase(1)
    first_sends(1, (2, 1, 3))
    pl.semaphore_wait(tok.at[0], 2)
    token(tok, 1, (2, -2), zpeer, c)
    first_phase(2)
    first_sends(2, (2,))
    first_phase(3)
    second_phase(0)
    first_sends(2, (1, 3))
    first_sends(3, (2, 1, 3))
    pl.semaphore_wait(tok.at[1], 2)
    token(tok, 2, (4, -4), zpeer, c)
    gram_send(0)
    second_phase(1)
    wait(cw_ref, load_sem.at[7])
    cw = cw_ref[pl.ds(q, 1), :]
    scale = jnp.where(lax.broadcasted_iota(jnp.int32, (1, 128), 1) // 64 == core, cw, pltpu.roll(cw, 64, 1))
    pl.semaphore_wait(tok.at[2], 2)
    exchange(0)
    second_phase(2)
    exchange(1)
    gram_add(0)
    gram_send(1)
    second_phase(3)
    exchange(2)
    for p in range(2):
        vt[p] = v_buf[p].T
    exchange(3)
    wait(t_buf, load_sem.at[2])
    w2[...] = lax.dot_general(t_buf[1].astype(BF16), vt[1], TA, preferred_element_type=F32).astype(BF16)

    wait(cbuf.at[pl.ds(0, NZ - 1)], z_sem.at[1])
    cur = cbuf[...].astype(F32)
    turned = pltpu.roll(cur.reshape(256, 128), 64, 1).reshape(NZ, 16, 128)
    left = lax.broadcasted_iota(jnp.int32, (NZ, 16, 128), 2) < 64
    own = jnp.stack([jnp.where(left, cur, turned), jnp.where(left, turned, cur)], axis=1).reshape(512, 128)
    own16 = own.astype(BF16)
    low = lax.broadcasted_iota(jnp.int32, (256, 128), 1) < 64
    proj = jnp.where(low, dot(vt[0], own16), dot(vt[1], own16)).reshape(8, 32, 128)
    pf[...] = proj
    ps[...] = proj.astype(BF16)
    for j, d in enumerate(NEAR):
        send(ps.at[zpeer(d) & 7], pr.at[j], p_sem.at[0], p_sem.at[1], (zpeer(d), c))

    for b in range(4):
        own_t[:, b * 128 : b * 128 + 128] = own[b * 128 : b * 128 + 128].T[:64]
    gram_add(1)
    gall[core, q] = gsum[2].astype(BF16)
    for dy in range(NY):
        for dx in range(NX):
            if dx or dy:
                dest = (((y + dy) & (NY - 1)) * NX + ((x + dx) & (NX - 1))) * 2 + core
                send(gall.at[core, q], gall.at[core, q], g_sem.at[4], g_sem.at[5], (z, dest))

    wait(pr, p_sem.at[1])
    total = pf[z & 7]
    for j in range(len(NEAR)):
        total += pr[j].astype(F32)
    pall[z] = total.astype(BF16)
    for d in DIST[:-1]:
        send(pall.at[z], pall.at[z], p_sem.at[2], p_sem.at[3], (zpeer(d), c))
    wait(gall.at[0, pl.ds(0, NQ - 1)], g_sem.at[5])
    send(gall.at[core], gall.at[core], gx_sem.at[0], gx_sem.at[1], mate)
    wait(gall.at[0], gx_sem.at[1])
    rest = jnp.concatenate(
        [
            lax.dot_general(gall[k].reshape(256, 128), w2[...], TA, preferred_element_type=F32)
            for k in range(2)
        ],
        axis=0,
    )
    rest = (vt[0].astype(F32) - rest).astype(BF16)
    w1[...] = lax.dot_general(t_buf[0].astype(BF16), rest, TA, preferred_element_type=F32).astype(BF16)

    for t in range(NT):
        wait(precv.at[t], pair_s.at[t])
        wait(r1.at[t], s1_s.at[t])
        wait(r2.at[t], s2_s.at[t])
    for i in range(2):
        wait(gin.at[i], g_sem.at[i])
    wait(gall.at[0, pl.ds(0, NQ - 1)], g_sem.at[4])
    wait(gall.at[0], gx_sem.at[0])
    wait(cbuf.at[pl.ds(0, NZ - 1)], z_sem.at[0])
    wait(pr, p_sem.at[0])
    wait(pall.at[pl.ds(0, NZ - 1)], p_sem.at[2])
    wait(pall.at[pl.ds(0, NZ - 1)], p_sem.at[3])
    proj = (pall[:8].astype(F32) + pall[8:].astype(F32)).reshape(256, 128).T.astype(BF16)
    out_ref[...] = (own_t[...] - (dot(proj[:64], w1[...]) + dot(proj[64:], w2[...]))).astype(BF16)


def token(tok, at, steps, zpeer, c):
    for d in steps:
        pl.semaphore_signal(tok.at[at], inc=1, device_id=(zpeer(d), c), device_id_type=MESH)


def shards(a, order, weight, gap, shift, cw, v, t):
    hbm = pl.BlockSpec(memory_space=pl.ANY)
    dma = pltpu.SemaphoreType.DMA
    vmem = pltpu.VMEM
    out = pl.pallas_call(
        kernel,
        out_shape=vmem((64, 512), BF16),
        in_specs=[hbm] * 8,
        out_specs=pl.BlockSpec(memory_space=pltpu.VMEM),
        scratch_shapes=[
            vmem((1, 512), jnp.int32), vmem((1, 512), F32), vmem((NQ, 128), jnp.int32),
            vmem((NQ, 128), F32), vmem((NQ, 128), F32),
            vmem((NT, 2, 4, 16, 512), BF16),
            vmem((2, 512, 256), BF16),
            vmem((2, 256, 256), F32),
            vmem((2, 256, 512), BF16),
            vmem((4, 128, 128), F32),
            vmem((4, 128, 128), F32),
            vmem((4, 512, 512), BF16),
            vmem((2, NT, 8, 128, 128), BF16),
            vmem((NT, 8, 128, 128), BF16),
            vmem((NT, 2, 4, 4, 32, 128), BF16),
            vmem((NT, 2, 3, 4, 32, 128), BF16),
            vmem((NT, 2, 4, 32, 128), BF16),
            vmem((NT, 2, 3, 32, 128), BF16),
            vmem((NT, 4, 16, 128), BF16),
            vmem((NZ, 16, 128), BF16),
            vmem((NQ, 16, 128), F32),
            vmem((3, 16, 128), F32),
            vmem((2, 3, 16, 128), F32),
            vmem((2, NQ, 16, 128), BF16),
            vmem((256, 512), BF16),
            vmem((256, 512), BF16),
            vmem((64, 512), F32),
            vmem((8, 32, 128), F32),
            vmem((8, 32, 128), BF16),
            vmem((7, 32, 128), BF16),
            vmem((NZ, 32, 128), BF16),
            dma((8,)), dma((NT,)), dma((NT,)), dma((NT,)), dma((NT,)), dma((NT,)), dma((NT,)),
            dma((2,)), dma((10,)), dma((2,)), dma((4,)), pltpu.SemaphoreType.REGULAR((3,)),
        ],
        compiler_params=pltpu.CompilerParams(collective_id=0, has_side_effects=True),
    )(
        a.reshape(NZ, 2, 16, 512), order.reshape(1, -1), weight.reshape(1, -1), gap.reshape(NQ, 128),
        shift.reshape(NQ, 128), cw.reshape(NQ, 128), v, t,
    )
    return out.T


def solution(mesh):
    return jax.shard_map(
        shards,
        mesh=mesh,
        in_specs=(P("row", "col"), P("col"), P("col"), P(), P(), P(), P(None, "row", None), P()),
        out_specs=P("row", "col"),
        check_vma=False,
    )
```

time: 132 us -> 46.3 us (0.35)
  the two profiles are of different devices: /device:TPU:32 before, /device:TPU:8 now
where the time goes in v2:
time: 46.3 us; the launch traced here: 46.2 us
  Pallas kernels  45.5 us (98%)
  local copies, waits for them, and re-layouts  0.63 us (1%)
    pallas_call x1, Pallas kernels, shards(): pl.pallas_call(kernel, out_shape=vmem((64, 512), BF16), in_specs=[hbm] *...  45.5 us

profile of v2, /device:TPU:8, one launch (start us, length us, event | category | flops | bytes accessed | tf_op | source)
XLA Modules:
  0.0 46.2 jit_solution(2044782212361975009)
XLA Ops:
  0.0 45.5 %shard_map.82 = bf16[64,512]{1,0:T(8,128)(2,1)S(1)} custom-call(bf16[16,2,16,512]{3,2,1,0:T(8,128)(2,1)} %bitcast.8, s32[1,512]{1,0:T(1,128)} %bitcast.12, f32[1,512]{1,0:T(1,128)} %bitcast.13, s32[16,128]{1,0:T(8,128)} %bitcast.9, f32[16,128]{1,0:T(8,128)} %bitcast.10, f32[16,128]{1,0:T(8,128)} %bitcast.11, bf16[2,512,256]{2,1,0:T(8,128)(2,1)} %v_hbm.1, ...), custom_call_target="tpu_custom_call" | custom-call | tf_op jit(solution)/shard_map/pallas_call | solution.py:271
  45.5 0.6 %copy.10 = bf16[512,64]{0,1:T(8,128)(2,1)} copy(bf16[512,64]{0,1:T(8,128)(2,1)S(1)} %bitcast.7) | data formatting | bytes 131072

commit v3 on v2

--- a/solution.py
+++ b/solution.py
@@ -10,7 +10,8 @@
 NZ, NX, NY = 16, 4, 4
 NQ = NX * NY
 DIST = [8] + [s * d for d in range(7, 0, -1) for s in (1, -1)] + [0]
-NEAR = [4, 3, -3, 2, -2, 1, -1]
+GATHER = [0, 1, 2, 3, 4, 5, 6, 15, 14, 7, 13, 12, 11, 8, 10, 9]
+OWNERS = [4, 13, 3, 14, 2, 15, 1, 0]
 NT = 4
 TA = (((0,), (0,)), ((), ()))
 
@@ -126,8 +127,7 @@
     def first_phase(t):
         wait(precv.at[t], pair_r.at[t])
 
-        @pl.loop(0, NY)
-        def _(yy):
+        for yy in range(NY):
             for e in range(2):
                 total = part[core, t, 2 * yy + e].astype(F32) + precv[t, 2 * yy + e].astype(F32)
                 turned = pltpu.roll(total, 64, 1)
@@ -167,17 +167,13 @@
             else:
                 cbuf[z] = mz[t, i]
 
-    first_phase(0)
-    first_sends(0, (2, 1, 3))
-    first_phase(1)
-    first_sends(1, (2, 1, 3))
+    for t in range(3):
+        first_phase(t)
+        first_sends(t, (2, 1, 3))
     pl.semaphore_wait(tok.at[0], 2)
     token(tok, 1, (2, -2), zpeer, c)
-    first_phase(2)
-    first_sends(2, (2,))
+    second_phase(0)
     first_phase(3)
-    second_phase(0)
-    first_sends(2, (1, 3))
     first_sends(3, (2, 1, 3))
     pl.semaphore_wait(tok.at[1], 2)
     token(tok, 2, (4, -4), zpeer, c)
@@ -194,9 +190,9 @@
     gram_send(1)
     second_phase(3)
     exchange(2)
+    exchange(3)
     for p in range(2):
         vt[p] = v_buf[p].T
-    exchange(3)
     wait(t_buf, load_sem.at[2])
     w2[...] = lax.dot_general(t_buf[1].astype(BF16), vt[1], TA, preferred_element_type=F32).astype(BF16)
 
@@ -210,8 +206,16 @@
     proj = jnp.where(low, dot(vt[0], own16), dot(vt[1], own16)).reshape(8, 32, 128)
     pf[...] = proj
     ps[...] = proj.astype(BF16)
-    for j, d in enumerate(NEAR):
-        send(ps.at[zpeer(d) & 7], pr.at[j], p_sem.at[0], p_sem.at[1], (zpeer(d), c))
+    slot = (z + 3) & (NZ - 1)
+    for owner in OWNERS:
+
+        @pl.when(z != owner)
+        def _(owner=owner):
+            send(
+                ps.at[(owner + 3) % NZ], pr.at[(z - owner - 1 + NZ) & (NZ - 1)],
+                p_sem.at[0], p_sem.at[1], (owner, c),
+            )
+
 
     for b in range(4):
         own_t[:, b * 128 : b * 128 + 128] = own[b * 128 : b * 128 + 128].T[:64]
@@ -223,13 +227,19 @@
                 dest = (((y + dy) & (NY - 1)) * NX + ((x + dx) & (NX - 1))) * 2 + core
                 send(gall.at[core, q], gall.at[core, q], g_sem.at[4], g_sem.at[5], (z, dest))
 
-    wait(pr, p_sem.at[1])
-    total = pf[z & 7]
-    for j in range(len(NEAR)):
-        total += pr[j].astype(F32)
-    pall[z] = total.astype(BF16)
-    for d in DIST[:-1]:
-        send(pall.at[z], pall.at[z], p_sem.at[2], p_sem.at[3], (zpeer(d), c))
+    @pl.when(slot < 8)
+    def _():
+        wait(pr, p_sem.at[1])
+        total = pf[slot]
+        for j in range(NZ - 1):
+            total += pr[j].astype(F32)
+        pall[slot] = total.astype(BF16)
+        for dest in GATHER:
+
+            @pl.when(z != dest)
+            def _(dest=dest):
+                send(pall.at[slot], pall.at[slot], p_sem.at[2], p_sem.at[3], (dest, c))
+
     wait(gall.at[0, pl.ds(0, NQ - 1)], g_sem.at[5])
     send(gall.at[core], gall.at[core], gx_sem.at[0], gx_sem.at[1], mate)
     wait(gall.at[0], gx_sem.at[1])
@@ -252,10 +262,19 @@
     wait(gall.at[0, pl.ds(0, NQ - 1)], g_sem.at[4])
     wait(gall.at[0], gx_sem.at[0])
     wait(cbuf.at[pl.ds(0, NZ - 1)], z_sem.at[0])
-    wait(pr, p_sem.at[0])
-    wait(pall.at[pl.ds(0, NZ - 1)], p_sem.at[2])
-    wait(pall.at[pl.ds(0, NZ - 1)], p_sem.at[3])
-    proj = (pall[:8].astype(F32) + pall[8:].astype(F32)).reshape(256, 128).T.astype(BF16)
+
+    @pl.when(slot < 8)
+    def _():
+        wait(pr.at[pl.ds(0, 7)], p_sem.at[0])
+        wait(pr, p_sem.at[2])
+        wait(pall.at[pl.ds(0, 7)], p_sem.at[3])
+
+    @pl.when(slot >= 8)
+    def _():
+        wait(pr.at[pl.ds(0, 8)], p_sem.at[0])
+        wait(pall, p_sem.at[3])
+
+    proj = pall[...].reshape(256, 128).T
     out_ref[...] = (own_t[...] - (dot(proj[:64], w1[...]) + dot(proj[64:], w2[...]))).astype(BF16)
 
 
@@ -300,8 +319,8 @@
             vmem((64, 512), F32),
             vmem((8, 32, 128), F32),
             vmem((8, 32, 128), BF16),
-            vmem((7, 32, 128), BF16),
-            vmem((NZ, 32, 128), BF16),
+            vmem((NZ - 1, 32, 128), BF16),
+            vmem((8, 32, 128), BF16),
             dma((8,)), dma((NT,)), dma((NT,)), dma((NT,)), dma((NT,)), dma((NT,)), dma((NT,)),
             dma((2,)), dma((10,)), dma((2,)), dma((4,)), pltpu.SemaphoreType.REGULAR((3,)),
         ],

time: 46.3 us -> 44.8 us (0.968)
  the two profiles are of different devices: /device:TPU:8 before, /device:TPU:64 now
where the time goes in v3:
time: 44.8 us; the launch traced here: 44.6 us
  Pallas kernels  44 us (98%)
  local copies, waits for them, and re-layouts  0.63 us (1%)
    pallas_call x1, Pallas kernels, shards(): pl.pallas_call(kernel, out_shape=vmem((64, 512), BF16), in_specs=[hbm] *...  44 us

profile of v3, /device:TPU:64, one launch (start us, length us, event | category | flops | bytes accessed | tf_op | source)
XLA Modules:
  0.0 44.6 jit_solution(2020516531867004894)
XLA Ops:
  0.0 44.0 %shard_map.82 = bf16[64,512]{1,0:T(8,128)(2,1)S(1)} custom-call(bf16[16,2,16,512]{3,2,1,0:T(8,128)(2,1)} %bitcast.8, s32[1,512]{1,0:T(1,128)} %bitcast.12, f32[1,512]{1,0:T(1,128)} %bitcast.13, s32[16,128]{1,0:T(8,128)} %bitcast.9, f32[16,128]{1,0:T(8,128)} %bitcast.10, f32[16,128]{1,0:T(8,128)} %bitcast.11, bf16[2,512,256]{2,1,0:T(8,128)(2,1)} %v_hbm.1, ...), custom_call_target="tpu_custom_call" | custom-call | tf_op jit(solution)/shard_map/pallas_call | solution.py:290
  44.0 0.6 %copy.10 = bf16[512,64]{0,1:T(8,128)(2,1)} copy(bf16[512,64]{0,1:T(8,128)(2,1)S(1)} %bitcast.7) | data formatting | bytes 131072

commit v4 on v3

--- a/solution.py
+++ b/solution.py
@@ -24,7 +24,7 @@
     a_hbm, order_hbm, weight_hbm, gap_hbm, shift_hbm, cw_hbm, v_hbm, t_hbm, out_ref,
     order_ref, weight_ref, gap_ref, shift_ref, cw_ref, a_buf, v_buf, t_buf, vt,
     pole_b, weight_b, cau, part, precv, s1, r1, s2, r2, mz, cbuf,
-    gf, gsum, gin, gall, w1, w2, own_t, pf, ps, pr, pall,
+    gf, gsum, gout, gin, gall, w1, w2, own_t, pf, ps, pr, pall,
     load_sem, pair_s, pair_r, s1_s, s1_r, s2_s, s2_r, z_sem, g_sem, gx_sem, p_sem, tok,
 ):
     z = lax.axis_index("row")
@@ -104,7 +104,7 @@
                 part[n // 2, t, 4 * (n % 2) + e] = prod[:, e * 128 : e * 128 + 128]
         if t == 0:
             pl.semaphore_wait(barrier, len(peers))
-        send(part.at[1 - core, t], precv.at[t], pair_s.at[t], pair_r.at[t], mate)
+        send(part.at[1 - core, t], precv.at[t], pair_s, pair_r.at[t], mate)
     token(tok, 0, (1, -1), zpeer, c)
 
     wait(v_buf, load_sem.at[1])
@@ -114,13 +114,14 @@
     gsum[0] = gf[q]
 
     def gram_send(i):
+        gout[i] = gsum[i].astype(BF16)
         for j in range(3):
             to = zpeer((1 - 2 * core) * (j + 1) * 4**i)
-            send(gsum.at[i], gin.at[i, j], g_sem.at[i], g_sem.at[2 + i], (to, c))
+            send(gout.at[i], gin.at[i, j], g_sem.at[i], g_sem.at[2 + i], (to, c))
 
     def gram_add(i):
         wait(gin.at[i], g_sem.at[2 + i])
-        gsum[i + 1] = gsum[i] + gin[i, 0] + gin[i, 1] + gin[i, 2]
+        gsum[i + 1] = gsum[i] + gin[i, 0].astype(F32) + gin[i, 1].astype(F32) + gin[i, 2].astype(F32)
 
     left64 = lax.broadcasted_iota(jnp.int32, (64, 128), 1) < 64
 
@@ -139,8 +140,8 @@
 
     def first_sends(t, ds):
         for d in ds:
-            send(s1.at[t, 0, (x + d) & (NX - 1)], r1.at[t, 0, d - 1], s1_s.at[t], s1_r.at[t], (z, xchip(d)))
-            send(s1.at[t, 1, (y + d) & (NY - 1)], r1.at[t, 1, d - 1], s1_s.at[t], s1_r.at[t], (z, ychip(d)))
+            send(s1.at[t, 0, (x + d) & (NX - 1)], r1.at[t, 0, d - 1], s1_s, s1_r.at[t], (z, xchip(d)))
+            send(s1.at[t, 1, (y + d) & (NY - 1)], r1.at[t, 1, d - 1], s1_s, s1_r.at[t], (z, ychip(d)))
 
     def second_phase(t):
         wait(r1.at[t], s1_r.at[t])
@@ -150,8 +151,8 @@
                 total += r1[t, h, j].astype(F32)
             s2[t, h] = total.astype(BF16)
         for d in (2, 1, 3):
-            send(s2.at[t, 0, ((y + d) & (NY - 1))], r2.at[t, 0, d - 1], s2_s.at[t], s2_r.at[t], (z, ychip(d)))
-            send(s2.at[t, 1, ((x + d) & (NX - 1))], r2.at[t, 1, d - 1], s2_s.at[t], s2_r.at[t], (z, xchip(d)))
+            send(s2.at[t, 0, ((y + d) & (NY - 1))], r2.at[t, 0, d - 1], s2_s, s2_r.at[t], (z, ychip(d)))
+            send(s2.at[t, 1, ((x + d) & (NX - 1))], r2.at[t, 1, d - 1], s2_s, s2_r.at[t], (z, xchip(d)))
 
     def exchange(t):
         wait(r2.at[t], s2_r.at[t])
@@ -172,6 +173,9 @@
         first_sends(t, (2, 1, 3))
     pl.semaphore_wait(tok.at[0], 2)
     token(tok, 1, (2, -2), zpeer, c)
+    wait(cw_ref, load_sem.at[7])
+    cw = cw_ref[pl.ds(q, 1), :]
+    scale = jnp.where(lax.broadcasted_iota(jnp.int32, (1, 128), 1) // 64 == core, cw, pltpu.roll(cw, 64, 1))
     second_phase(0)
     first_phase(3)
     first_sends(3, (2, 1, 3))
@@ -179,9 +183,6 @@
     token(tok, 2, (4, -4), zpeer, c)
     gram_send(0)
     second_phase(1)
-    wait(cw_ref, load_sem.at[7])
-    cw = cw_ref[pl.ds(q, 1), :]
-    scale = jnp.where(lax.broadcasted_iota(jnp.int32, (1, 128), 1) // 64 == core, cw, pltpu.roll(cw, 64, 1))
     pl.semaphore_wait(tok.at[2], 2)
     exchange(0)
     second_phase(2)
@@ -253,10 +254,9 @@
     rest = (vt[0].astype(F32) - rest).astype(BF16)
     w1[...] = lax.dot_general(t_buf[0].astype(BF16), rest, TA, preferred_element_type=F32).astype(BF16)
 
-    for t in range(NT):
-        wait(precv.at[t], pair_s.at[t])
-        wait(r1.at[t], s1_s.at[t])
-        wait(r2.at[t], s2_s.at[t])
+    wait(precv, pair_s)
+    wait(r1, s1_s)
+    wait(r2, s2_s)
     for i in range(2):
         wait(gin.at[i], g_sem.at[i])
     wait(gall.at[0, pl.ds(0, NQ - 1)], g_sem.at[4])
@@ -266,7 +266,6 @@
     @pl.when(slot < 8)
     def _():
         wait(pr.at[pl.ds(0, 7)], p_sem.at[0])
-        wait(pr, p_sem.at[2])
         wait(pall.at[pl.ds(0, 7)], p_sem.at[3])
 
     @pl.when(slot >= 8)
@@ -276,6 +275,10 @@
 
     proj = pall[...].reshape(256, 128).T
     out_ref[...] = (own_t[...] - (dot(proj[:64], w1[...]) + dot(proj[64:], w2[...]))).astype(BF16)
+
+    @pl.when(slot < 8)
+    def _():
+        wait(pr, p_sem.at[2])
 
 
 def token(tok, at, steps, zpeer, c):
@@ -312,7 +315,8 @@
             vmem((NZ, 16, 128), BF16),
             vmem((NQ, 16, 128), F32),
             vmem((3, 16, 128), F32),
-            vmem((2, 3, 16, 128), F32),
+            vmem((2, 16, 128), BF16),
+            vmem((2, 3, 16, 128), BF16),
             vmem((2, NQ, 16, 128), BF16),
             vmem((256, 512), BF16),
             vmem((256, 512), BF16),
@@ -321,7 +325,7 @@
             vmem((8, 32, 128), BF16),
             vmem((NZ - 1, 32, 128), BF16),
             vmem((8, 32, 128), BF16),
-            dma((8,)), dma((NT,)), dma((NT,)), dma((NT,)), dma((NT,)), dma((NT,)), dma((NT,)),
+            dma((8,)), dma, dma((NT,)), dma, dma((NT,)), dma, dma((NT,)),
             dma((2,)), dma((10,)), dma((2,)), dma((4,)), pltpu.SemaphoreType.REGULAR((3,)),
         ],
         compiler_params=pltpu.CompilerParams(collective_id=0, has_side_effects=True),

time: 44.8 us -> 45.2 us (level)
  the two profiles are of different devices: /device:TPU:64 before, /device:TPU:32 now
where the time goes in v4:
time: 45.2 us; the launch traced here: 45 us
  Pallas kernels  44.3 us (98%)
  local copies, waits for them, and re-layouts  0.63 us (1%)
    pallas_call x1, Pallas kernels, shards(): pl.pallas_call(kernel, out_shape=vmem((64, 512), BF16), in_specs=[hbm] *...  44.3 us

profile of v4, /device:TPU:32, one launch (start us, length us, event | category | flops | bytes accessed | tf_op | source)
XLA Modules:
  0.0 45.0 jit_solution(7704577201404958619)
XLA Ops:
  0.0 44.3 %shard_map.82 = bf16[64,512]{1,0:T(8,128)(2,1)S(1)} custom-call(bf16[16,2,16,512]{3,2,1,0:T(8,128)(2,1)} %bitcast.8, s32[1,512]{1,0:T(1,128)} %bitcast.12, f32[1,512]{1,0:T(1,128)} %bitcast.13, s32[16,128]{1,0:T(8,128)} %bitcast.9, f32[16,128]{1,0:T(8,128)} %bitcast.10, f32[16,128]{1,0:T(8,128)} %bitcast.11, bf16[2,512,256]{2,1,0:T(8,128)(2,1)} %v_hbm.1, ...), custom_call_target="tpu_custom_call" | custom-call | tf_op jit(solution)/shard_map/pallas_call | solution.py:293
  44.4 0.6 %copy.10 = bf16[512,64]{0,1:T(8,128)(2,1)} copy(bf16[512,64]{0,1:T(8,128)(2,1)S(1)} %bitcast.7) | data formatting | bytes 131072
